TPU v7x, 32 devices: a whole 2x2x4 slice. The times are simulated.
32 devices in a mesh: pos: 8 (over y, x, core), ang: 4 (over z).
Axes of the slice: x: 2, y: 2, z: 4, core: 2. Of those that a mesh axis runs over, the one named last changes fastest.
Arguments:
- object_field: float32 [2, 32, 256, 256], P(None, None, 'pos'), may hold values from -2.5 to 2.5
- probe_wave: float32 [2, 128, 128], replicated, may hold values from -4 to 4
- intensity: float32 [4, 32, 128, 128], P('ang', 'pos'), may hold values from 0.25 to 4
- positions: int32 [32, 2], P('pos'), may hold values from 0 to 255, as said below
- shear_steps: int32 [4, 32], replicated, may hold values from -8 to 8, as said below
Outputs:
- object_new: float32 [2, 32, 256, 256], P(None, None, 'pos')
Inputs may be any that keep to these rules, and one draw needn't show every extreme that they name: `positions`: row j is (column offset, row offset). With d = j // 4 and q = j mod 4: (column offset - d * 32 + 128 // 2) mod 256 lies in 0 .. 32; it is 0 for q = 0 and 32 for q = 1; the row offset lies in 0 .. 128, and is 128 for q = 0 and 0 for q = 1. For every angle a, shear_steps[a, 0] = -8 and shear_steps[a, 31] = 8.
All inputs are finite; a program needn't handle non-finite values.
Results may differ from a plain program's by a relative error of at most 0.0001.
Values sent between devices are 32-bit elements; how exact they have to be, the bound alone decides.
A program may use at most 64 MiB of HBM per device.

v0:
```python
import math
import jax
import jax.numpy as jnp
from jax import lax
from jax.sharding import PartitionSpec as P

FRAME = 128
Y = 256
SH = 8
ITERS = 3
MODULUS_FLOOR = 0.25
INTERSECTION_WEIGHT = 1.0
RELAXATION = 0.5
HIGHEST = lax.Precision.HIGHEST


def padded_2(block, sides, width):
    for axis, dim in sides:
        count = lax.axis_size(axis)
        forward = [(i, i + 1) for i in range(count - 1)]
        forward.append((count - 1, 0))
        backward = [(target, source) for source, target in forward]
        low = lax.ppermute(
            lax.slice_in_dim(block, block.shape[dim] - width, None, axis=dim), axis, forward
        )
        high = lax.ppermute(lax.slice_in_dim(block, 0, width, axis=dim), axis, backward)
        block = jnp.concatenate([low, block, high], axis=dim)
    return block


def passed_along(value, axis, steps):
    count = lax.axis_size(axis)
    pairs = [(source, (source + steps) % count) for source in range(count)]
    return lax.ppermute(value, axis, pairs)


def fourier_tables(length):
    indices = jnp.arange(length, dtype=jnp.int32)
    phases = (indices[:, None] * indices[None, :] % length).astype(jnp.float32) * (
        2.0 * math.pi / length
    )
    factor = 1.0 / math.sqrt(length)
    return (jnp.cos(phases) * factor, jnp.sin(phases) * factor)


def transform(real_part, imag_part, cosine, sine_table, exponent_sign):
    left_real = jnp.einsum(
        "jk,abkl->abjl", cosine, real_part, precision=HIGHEST
    ) - exponent_sign * jnp.einsum("jk,abkl->abjl", sine_table, imag_part, precision=HIGHEST)
    left_imag = jnp.einsum(
        "jk,abkl->abjl", cosine, imag_part, precision=HIGHEST
    ) + exponent_sign * jnp.einsum("jk,abkl->abjl", sine_table, real_part, precision=HIGHEST)
    out_real = jnp.einsum(
        "abjk,kl->abjl", left_real, cosine, precision=HIGHEST
    ) - exponent_sign * jnp.einsum("abjk,kl->abjl", left_imag, sine_table, precision=HIGHEST)
    out_imag = jnp.einsum(
        "abjk,kl->abjl", left_imag, cosine, precision=HIGHEST
    ) + exponent_sign * jnp.einsum("abjk,kl->abjl", left_real, sine_table, precision=HIGHEST)
    return (out_real, out_imag)


def deposit(target, get_piece, start_cols, start_rows, frame_total):
    leading = target.ndim - 2

    def add_one(frame_index, running):
        corner = (0,) * leading + (start_cols[frame_index], start_rows[frame_index])
        addition = get_piece(frame_index)
        current = lax.dynamic_slice(running, corner, addition.shape)
        return lax.dynamic_update_slice(running, current + addition, corner)

    return lax.fori_loop(0, frame_total, add_one, target)


def extract(source, start_cols, start_rows):
    leading = source.shape[:-2]

    def window_at(col_start, row_start):
        return lax.dynamic_slice(
            source, (0,) * len(leading) + (col_start, row_start), leading + (FRAME, FRAME)
        )

    return jax.vmap(window_at, out_axes=2)(start_cols, start_rows)


def per_device(object_field, probe_wave, intensity, positions, shear_steps):
    tile_width = object_field.shape[2]
    full_width = tile_width * lax.axis_size("pos")
    pos_index = lax.axis_index("pos")
    angle_count = intensity.shape[0]
    frame_total = positions.shape[0]
    angle_first = lax.axis_index("ang") * angle_count
    reach_tiles = -(-(FRAME // 2) // tile_width)
    band_count = 2 * reach_tiles + 1
    padded_width = tile_width + 2 * SH
    columns = jnp.arange(tile_width, dtype=jnp.int32)
    padded_cols = jnp.arange(padded_width, dtype=jnp.int32)
    my_steps = lax.dynamic_slice_in_dim(shear_steps, angle_first, angle_count, 0)
    padded = padded_2(object_field, (("pos", 2),), SH)
    forward_pick = (
        padded_cols[None, None, None, :]
        == columns[None, None, :, None] + SH + my_steps[:, :, None, None]
    ).astype(jnp.float32)
    projected = jnp.einsum("azxk,czky->acxy", forward_pick, padded, precision=HIGHEST)
    start_rows = positions[:, 1]
    start_cols = (positions[:, 0] - pos_index * tile_width + reach_tiles * tile_width) % full_width
    work_width = band_count * tile_width
    probe_real = probe_wave[0]
    probe_imag = probe_wave[1]
    probe_power = probe_real * probe_real + probe_imag * probe_imag
    cover_plane = deposit(
        jnp.zeros((work_width, Y), jnp.float32),
        lambda frame_index: probe_power,
        start_cols,
        start_rows,
        frame_total,
    )
    coverage = cover_plane[reach_tiles * tile_width : (reach_tiles + 1) * tile_width]
    for offset in range(band_count):
        if offset != reach_tiles:
            coverage = coverage + passed_along(
                cover_plane[offset * tile_width : (offset + 1) * tile_width],
                "pos",
                offset - reach_tiles,
            )
    cosine, sine_table = fourier_tables(FRAME)
    amplitude = jnp.sqrt(intensity)
    estimate = projected
    for iteration in range(ITERS):
        pieces = []
        for offset in range(band_count):
            if offset == reach_tiles:
                pieces.append(estimate)
            else:
                pieces.append(passed_along(estimate, "pos", reach_tiles - offset))
        source = jnp.concatenate(pieces, axis=2)
        patches = extract(source, start_cols, start_rows)
        patch_real = patches[:, 0]
        patch_imag = patches[:, 1]
        wave_real = probe_real * patch_real - probe_imag * patch_imag
        wave_imag = probe_real * patch_imag + probe_imag * patch_real
        freq_real, freq_imag = transform(wave_real, wave_imag, cosine, sine_table, -1.0)
        modulus = jnp.sqrt(freq_real * freq_real + freq_imag * freq_imag)
        factor = amplitude / jnp.maximum(modulus, MODULUS_FLOOR)
        exit_real, exit_imag = transform(
            freq_real * factor, freq_imag * factor, cosine, sine_table, 1.0
        )
        back_real = probe_real * exit_real + probe_imag * exit_imag
        back_imag = probe_real * exit_imag - probe_imag * exit_real
        contrib = jnp.stack([back_real, back_imag], axis=1)
        summed = deposit(
            jnp.zeros((angle_count, 2, work_width, Y), jnp.float32),
            lambda frame_index: contrib[:, :, frame_index],
            start_cols,
            start_rows,
            frame_total,
        )
        numerator = summed[:, :, reach_tiles * tile_width : (reach_tiles + 1) * tile_width]
        for offset in range(band_count):
            if offset != reach_tiles:
                numerator = numerator + passed_along(
                    summed[:, :, offset * tile_width : (offset + 1) * tile_width],
                    "pos",
                    offset - reach_tiles,
                )
        estimate = (numerator + INTERSECTION_WEIGHT * estimate) / (coverage + INTERSECTION_WEIGHT)
    change = estimate - projected
    change_rim = padded_2(change, (("pos", 2),), SH)
    every_rim = lax.all_gather(change_rim, "ang", axis=0, tiled=True)
    back_pick = (
        padded_cols[None, None, None, :]
        == columns[None, None, :, None] + SH - shear_steps[:, :, None, None]
    ).astype(jnp.float32)
    accumulated = jnp.einsum("azxk,acky->czxy", back_pick, every_rim, precision=HIGHEST)
    return object_field + RELAXATION / shear_steps.shape[0] * accumulated


def solution(mesh):
    placed = (P(None, None, "pos", None), P(), P("ang", "pos", None, None), P("pos", None), P())
    return jax.shard_map(
        per_device,
        mesh=mesh,
        in_specs=placed,
        out_specs=P(None, None, "pos", None),
        check_vma=False,
    )
```

profile of v0, /device:TPU:0, one launch (start us, length us, event | category | flops | bytes accessed | tf_op | source)
XLA Modules:
  0.0 269.1 jit_solution(3598538774012352433)
XLA Ops:
  0.0 2.3 fusion.380
  2.8 2.9 %collective-permute-start.1 = (f32[2,32,8,256]{3,2,1,0:T(8,128)S(1)}, f32[2,32,8,256]{3,2,1,0:T(8,128)}, u32[]{:S(2)}, u32[]{:S(2)}) collective-permute-start(f32[2,32,8,256]{3,2,1,0:T(8,128)S(1)} %get-tuple-element.525), channel_id=1, source_target_pairs={{4,0},{8,4},{12,8},{16,12},{20,16},{24,20},{28,24},{0,28},{5,1},{9... | collective-permute-start | bytes 1572872 | tf_op jit(solution)/shard_map/ppermute | solution.py:26
  6.8 25.6 %while.56 = (s32[]{:T(128)}, f32[160,256]{1,0:T(8,128)S(1)}, s32[4]{0:T(128)S(1)}, s32[4]{0:T(128)S(1)}, f32[128,128]{1,0:T(8,128)S(1)}, /*index=5*/s32[]{:T(128)}, s32[]{:T(128)}, s32[]{:T(128)}, s32[]{:T(128)}) while((s32[]{:T(128)}, f32[160,256]{1,0:T(8,128)S(1)}, s32[4]{0:T(128)S(1)}, s32[4]{0:T(128)S(1)}, f32[128,128]{1,0:T(8,128)S(1)}, ...), condition=%wide.region_3.4_spmd, body=%wide.region_2.3_spmd.sunk | while | flops 16392 | bytes 327877 | solution.py:71
  17.8 1.1 dynamic_update_slice.33
  24.0 1.7 dynamic_update_slice.33
  30.7 1.7 dynamic_update_slice.33
  33.1 2.4 collective-permute-start.10
  36.3 2.5 fusion.35
  38.8 2.0 collective-permute-start.2
  40.9 3.6 %collective-permute-done.2 = f32[1,2,32,256]{3,2,1,0:T(8,128)S(1)} collective-permute-done((f32[1,2,32,256]{3,2,1,0:T(8,128)S(1)}, f32[1,2,32,256]{3,2,1,0:T(8,128)S(1)}, u32[]{:S(2)}, u32[]{:S(2)}) %collective-permute-start.2) | collective-permute-done | bytes 65568 | tf_op jit(solution)/shard_map/ppermute | solution.py:34
  44.6 4.5 %collective-permute-done.3 = f32[1,2,32,256]{3,2,1,0:T(8,128)S(1)} collective-permute-done((f32[1,2,32,256]{3,2,1,0:T(8,128)S(1)}, f32[1,2,32,256]{3,2,1,0:T(8,128)S(1)}, u32[]{:S(2)}, u32[]{:S(2)}) %collective-permute-start.3) | collective-permute-done | bytes 65568 | tf_op jit(solution)/shard_map/ppermute | solution.py:34
  49.1 1.9 collective-permute-done.4
  51.7 3.6 %collective-permute-done.5 = f32[1,2,32,256]{3,2,1,0:T(8,128)S(1)} collective-permute-done((f32[1,2,32,256]{3,2,1,0:T(8,128)S(1)}, f32[1,2,32,256]{3,2,1,0:T(8,128)S(1)}, u32[]{:S(2)}, u32[]{:S(2)}) %collective-permute-start.5) | collective-permute-done | bytes 65568 | tf_op jit(solution)/shard_map/ppermute | solution.py:34
  55.3 8.7 %while.59 = (s32[]{:T(128)}, f32[1,2,160,256]{3,2,1,0:T(8,128)S(1)}, s32[4,4]{1,0:T(4,128)S(1)}, f32[4,1,2,128,128]{4,3,0,2,1:T(8,128)S(1)}, s32[]{:T(128)}) while((s32[]{:T(128)}, f32[1,2,160,256]{3,2,1,0:T(8,128)S(1)}, s32[4,4]{1,0:T(4,128)S(1)}, f32[4,1,2,128,128]{4,3,0,2,1:T(8,128)S(1)}, s32[]{:T(128)}) %tuple.172), condition=%wide.while_cond, body=%wide.while_body.sunk | while | flops 2 | bytes 262269 | solution.py:78
  56.0 1.4 bitcast_dynamic-update-slice_fusion.6
  58.0 1.4 bitcast_dynamic-update-slice_fusion.6
  60.1 1.4 bitcast_dynamic-update-slice_fusion.6
  62.1 1.4 bitcast_dynamic-update-slice_fusion.6
  76.2 29.0 %while.55 = (s32[]{:T(128)}, f32[1,2,160,256]{3,2,1,0:T(8,128)S(1)}, s32[4]{0:T(128)S(1)}, s32[4]{0:T(128)S(1)}, f32[1,2,4,128,128]{4,3,2,1,0:T(8,128)S(1)}, /*index=5*/s32[]{:T(128)}, s32[]{:T(128)}, s32[]{:T(128)}, s32[]{:T(128)}) while((s32[]{:T(128)}, f32[1,2,160,256]{3,2,1,0:T(8,128)S(1)}, s32[4]{0:T(128)S(1)}, s32[4]{0:T(128)S(1)}, ...), condition=%wide.region_1.2_spmd, body=%wide.region_0.1_spmd.sunk | while | flops 32776 | bytes 655561 | solution.py:71
  81.9 1.0 dynamic_update_slice.32
  88.5 1.2 dynamic_update_slice.32
  95.4 2.1 dynamic_update_slice.32
  103.1 2.1 dynamic_update_slice.32
  105.3 1.8 collective-permute-start.6
  107.1 1.1 collective-permute-start.7
  108.2 1.2 collective-permute-start.9
  110.6 2.3 collective-permute-done.8
  112.9 2.0 collective-permute-done.9
  115.1 2.6 collective-permute-start.16
  117.7 2.0 collective-permute-start.17
  120.4 1.8 collective-permute-done.17
  122.2 7.8 %while.60 = (s32[]{:T(128)}, f32[1,2,160,256]{3,2,1,0:T(8,128)S(1)}, s32[4,4]{1,0:T(4,128)S(1)}, f32[4,1,2,128,128]{4,3,0,2,1:T(8,128)S(1)}, s32[]{:T(128)}) while((s32[]{:T(128)}, f32[1,2,160,256]{3,2,1,0:T(8,128)S(1)}, s32[4,4]{1,0:T(4,128)S(1)}, f32[4,1,2,128,128]{4,3,0,2,1:T(8,128)S(1)}, s32[]{:T(128)}) %tuple.193), condition=%wide.while_cond.1, body=%wide.while_body.1.sunk | while | flops 2 | bytes 262269 | solution.py:78
  122.9 1.3 bitcast_dynamic-update-slice_fusion.7
  124.8 1.3 bitcast_dynamic-update-slice_fusion.7
  126.8 1.3 bitcast_dynamic-update-slice_fusion.7
  128.7 1.3 bitcast_dynamic-update-slice_fusion.7
  142.3 29.0 %while.57 = (s32[]{:T(128)}, f32[1,2,160,256]{3,2,1,0:T(8,128)S(1)}, s32[4]{0:T(128)S(1)}, s32[4]{0:T(128)S(1)}, f32[1,2,4,128,128]{4,3,2,1,0:T(8,128)S(1)}, /*index=5*/s32[]{:T(128)}, s32[]{:T(128)}, s32[]{:T(128)}, s32[]{:T(128)}) while((s32[]{:T(128)}, f32[1,2,160,256]{3,2,1,0:T(8,128)S(1)}, s32[4]{0:T(128)S(1)}, s32[4]{0:T(128)S(1)}, ...), condition=%wide.region_5.6_spmd, body=%wide.region_4.5_spmd.sunk | while | flops 32776 | bytes 655561 | solution.py:71
  154.6 1.2 dynamic_update_slice.34
  161.5 2.1 dynamic_update_slice.34
  169.2 2.1 dynamic_update_slice.34
  171.4 2.8 %collective-permute-start.18 = (f32[1,2,32,256]{3,2,1,0:T(8,128)S(1)}, f32[1,2,32,256]{3,2,1,0:T(8,128)S(1)}, u32[]{:S(2)}, u32[]{:S(2)}) collective-permute-start(f32[1,2,32,256]{3,2,1,0:T(8,128)S(1)} %get-tuple-element.542), channel_id=1, source_target_pairs={{0,24},{4,28},{8,0},{12,4},{16,8},{20,12},{24,16},{28,20},{1,25},{... | collective-permute-start | bytes 196616 | tf_op jit(solution)/shard_map/ppermute | solution.py:34
  174.7 1.8 collective-permute-done.18
  176.5 1.4 collective-permute-done.19
  178.8 1.4 collective-permute-done.21
  181.2 2.6 collective-permute-start.24
  183.8 1.1 collective-permute-start.25
  186.2 1.9 collective-permute-done.25
  188.2 8.2 %while.61 = (s32[]{:T(128)}, f32[1,2,160,256]{3,2,1,0:T(8,128)S(1)}, s32[4,4]{1,0:T(4,128)S(1)}, f32[4,1,2,128,128]{4,3,0,2,1:T(8,128)S(1)}, s32[]{:T(128)}) while((s32[]{:T(128)}, f32[1,2,160,256]{3,2,1,0:T(8,128)S(1)}, s32[4,4]{1,0:T(4,128)S(1)}, f32[4,1,2,128,128]{4,3,0,2,1:T(8,128)S(1)}, s32[]{:T(128)}) %tuple.194), condition=%wide.while_cond.2, body=%wide.while_body.2.sunk | while | flops 2 | bytes 262269 | solution.py:78
  188.8 1.4 bitcast_dynamic-update-slice_fusion.8
  190.9 1.4 bitcast_dynamic-update-slice_fusion.8
  192.9 1.4 bitcast_dynamic-update-slice_fusion.8
  195.0 1.4 bitcast_dynamic-update-slice_fusion.8
  208.7 29.0 %while.58 = (s32[]{:T(128)}, f32[1,2,160,256]{3,2,1,0:T(8,128)S(1)}, s32[4]{0:T(128)S(1)}, s32[4]{0:T(128)S(1)}, f32[1,2,4,128,128]{4,3,2,1,0:T(8,128)S(1)}, /*index=5*/s32[]{:T(128)}, s32[]{:T(128)}, s32[]{:T(128)}, s32[]{:T(128)}) while((s32[]{:T(128)}, f32[1,2,160,256]{3,2,1,0:T(8,128)S(1)}, s32[4]{0:T(128)S(1)}, s32[4]{0:T(128)S(1)}, ...), condition=%wide.region_7.8_spmd, body=%wide.region_6.7_spmd.sunk | while | flops 32776 | bytes 655561 | solution.py:71
  221.0 1.2 dynamic_update_slice.35
  227.8 2.1 dynamic_update_slice.35
  235.6 2.1 dynamic_update_slice.35
  237.8 2.2 collective-permute-start.26
  240.5 1.7 collective-permute-done.26
  242.2 1.4 collective-permute-done.27
  244.5 1.4 collective-permute-done.29
  246.0 2.6 collective-permute-start.31
  248.8 1.3 collective-permute-done.30
  250.1 15.1 %all_gather.3 = f32[4,2,48,256]{3,2,1,0:T(8,128)S(1)} all-gather(f32[1,2,48,256]{3,2,1,0:T(8,128)S(1)} %pad_maximum_fusion.3), channel_id=1, replica_groups=mesh['pos'=8,'ang'=4] {'ang'}, dimensions={0}, use_global_device_ids=true | all-gather | bytes 491520 | tf_op jit(solution)/shard_map/all_gather | solution.py:168
  265.2 3.6 %bitcast_add_fusion.3 = f32[2,32,32,256]{3,2,1,0:T(8,128)} fusion(f32[2,32,32,256]{3,2,1,0:T(8,128)S(1)} %copy-done, s32[4,32,32]{2,0,1:T(4,128)S(1)} %broadcast_subtract_fusion, f32[4,2,48,256]{3,2,1,0:T(8,128)S(1)} %all_gather.3), kind=kOutput, calls=%fused_computation.16 | convolution fusion | flops 1209204736 | bytes 4603904 | tf_op jit(solution)/shard_map/azxk,acky->czxy/dot_general | solution.py:173
  (228 shorter events, 81.3 us)
Async XLA Ops:
  0.0 36.3 %copy-start = (f32[2,32,32,256]{3,2,1,0:T(8,128)S(1)}, f32[2,32,32,256]{3,2,1,0:T(8,128)}, u32[]{:S(2)}) copy-start(f32[2,32,32,256]{3,2,1,0:T(8,128)} %param.13) | copy-start | bytes 6291460
  0.0 5.6 %copy-start.3 = (s32[4,2]{0,1:T(2,128)S(1)}, s32[4,2]{0,1:T(2,128)}, u32[]{:S(2)}) copy-start(s32[4,2]{0,1:T(2,128)} %param.16) | copy-start | bytes 100
  0.0 36.2 %copy-start.1 = (f32[2,128,128]{2,1,0:T(8,128)S(1)}, f32[2,128,128]{2,1,0:T(8,128)}, u32[]{:S(2)}) copy-start(f32[2,128,128]{2,1,0:T(8,128)} %param.14) | copy-start | bytes 393220
  0.0 36.1 %copy-start.2 = (s32[4,32]{1,0:T(4,128)S(1)}, s32[4,32]{1,0:T(4,128)}, u32[]{:S(2)}) copy-start(s32[4,32]{1,0:T(4,128)} %param.17) | copy-start | bytes 1540
  2.3 33.9 %collective-permute-start = (f32[2,32,8,256]{3,2,1,0:T(8,128)}, f32[2,32,8,256]{3,2,1,0:T(8,128)}, u32[]{:S(2)}, u32[]{:S(2)}) collective-permute-start(f32[2,32,8,256]{3,2,1,0:T(8,128)} %get-tuple-element.524), channel_id=1, source_target_pairs={{0,4},{4,8},{8,12},{12,16},{16,20},{20,24},{24,28},{28,0},{1,5},{5... | collective-permute-start | bytes 1572872 | tf_op jit(solution)/shard_map/ppermute | solution.py:23
  2.8 33.5 %collective-permute-start.1 = (f32[2,32,8,256]{3,2,1,0:T(8,128)S(1)}, f32[2,32,8,256]{3,2,1,0:T(8,128)}, u32[]{:S(2)}, u32[]{:S(2)}) collective-permute-start(f32[2,32,8,256]{3,2,1,0:T(8,128)S(1)} %get-tuple-element.525), channel_id=1, source_target_pairs={{4,0},{8,4},{12,8},{16,12},{20,16},{24,20},{28,24},{0,28},{5,1},{9... | collective-permute-start | bytes 1572872 | tf_op jit(solution)/shard_map/ppermute | solution.py:26
  33.1 74.0 %collective-permute-start.10 = (f32[32,256]{1,0:T(8,128)}, f32[32,256]{1,0:T(8,128)S(1)}, u32[]{:S(2)}, u32[]{:S(2)}) collective-permute-start(f32[32,256]{1,0:T(8,128)} %get-tuple-element.550), channel_id=1, source_target_pairs={{0,24},{4,28},{8,0},{12,4},{16,8},{20,12},{24,16},{28,20},{1,25},{... | collective-permute-start | bytes 98312 | tf_op jit(solution)/shard_map/ppermute | solution.py:34
  35.5 72.8 %collective-permute-start.11 = (f32[32,256]{1,0:T(8,128)}, f32[32,256]{1,0:T(8,128)S(1)}, u32[]{:S(2)}, u32[]{:S(2)}) collective-permute-start(f32[32,256]{1,0:T(8,128)} %get-tuple-element.553), channel_id=1, source_target_pairs={{0,28},{4,0},{8,4},{12,8},{16,12},{20,16},{24,20},{28,24},{1,29},{... | collective-permute-start | bytes 98312 | tf_op jit(solution)/shard_map/ppermute | solution.py:34
  35.5 72.8 %collective-permute-start.12 = (f32[32,256]{1,0:T(8,128)}, f32[32,256]{1,0:T(8,128)}, u32[]{:S(2)}, u32[]{:S(2)}) collective-permute-start(f32[32,256]{1,0:T(8,128)} %get-tuple-element.552), channel_id=1, source_target_pairs={{0,4},{4,8},{8,12},{12,16},{16,20},{20,24},{24,28},{28,0},{1,5},{5... | collective-permute-start | bytes 98312 | tf_op jit(solution)/shard_map/ppermute | solution.py:34
  36.2 73.3 %collective-permute-start.13 = (f32[32,256]{1,0:T(8,128)}, f32[32,256]{1,0:T(8,128)}, u32[]{:S(2)}, u32[]{:S(2)}) collective-permute-start(f32[32,256]{1,0:T(8,128)} %get-tuple-element.551), channel_id=1, source_target_pairs={{0,8},{4,12},{8,16},{12,20},{16,24},{20,28},{24,0},{28,4},{1,9},{5... | collective-permute-start | bytes 98312 | tf_op jit(solution)/shard_map/ppermute | solution.py:34
  38.8 5.6 %collective-permute-start.2 = (f32[1,2,32,256]{3,2,1,0:T(8,128)S(1)}, f32[1,2,32,256]{3,2,1,0:T(8,128)S(1)}, u32[]{:S(2)}, u32[]{:S(2)}) collective-permute-start(f32[1,2,32,256]{3,2,1,0:T(8,128)S(1)} %fusion.35), channel_id=1, source_target_pairs={{0,8},{4,12},{8,16},{12,20},{16,24},{20,28},{24,0},{28,4},{1,9},{5... | collective-permute-start | bytes 196616 | tf_op jit(solution)/shard_map/ppermute | solution.py:34
  44.5 4.6 %collective-permute-start.3 = (f32[1,2,32,256]{3,2,1,0:T(8,128)S(1)}, f32[1,2,32,256]{3,2,1,0:T(8,128)S(1)}, u32[]{:S(2)}, u32[]{:S(2)}) collective-permute-start(f32[1,2,32,256]{3,2,1,0:T(8,128)S(1)} %fusion.35), channel_id=1, source_target_pairs={{0,4},{4,8},{8,12},{12,16},{16,20},{20,24},{24,28},{28,0},{1,5},{5... | collective-permute-start | bytes 196616 | tf_op jit(solution)/shard_map/ppermute | solution.py:34
  49.0 1.9 collective-permute-start.4
  51.0 4.3 %collective-permute-start.5 = (f32[1,2,32,256]{3,2,1,0:T(8,128)S(1)}, f32[1,2,32,256]{3,2,1,0:T(8,128)S(1)}, u32[]{:S(2)}, u32[]{:S(2)}) collective-permute-start(f32[1,2,32,256]{3,2,1,0:T(8,128)S(1)} %fusion.35), channel_id=1, source_target_pairs={{0,24},{4,28},{8,0},{12,4},{16,8},{20,12},{24,16},{28,20},{1,25},{... | collective-permute-start | bytes 196616 | tf_op jit(solution)/shard_map/ppermute | solution.py:34
  64.8 4.5 %copy-start.4 = (f32[1,4,128,128]{3,2,1,0:T(8,128)S(1)}, f32[1,4,128,128]{3,2,1,0:T(8,128)}, u32[]{:S(2)}) copy-start(f32[1,4,128,128]{3,2,1,0:T(8,128)} %param.15) | copy-start | bytes 786436
  105.3 4.2 %copy-start.7 = (s32[4]{0:T(128)}, s32[4]{0:T(128)S(1)}, u32[]{:S(2)}) copy-start(s32[4]{0:T(128)S(1)} %get-tuple-element.988) | copy-start | bytes 52
  105.3 5.0 %collective-permute-start.6 = (f32[1,2,32,256]{3,2,1,0:T(8,128)S(1)}, f32[1,2,32,256]{3,2,1,0:T(8,128)S(1)}, u32[]{:S(2)}, u32[]{:S(2)}) collective-permute-start(f32[1,2,32,256]{3,2,1,0:T(8,128)S(1)} %get-tuple-element.546), channel_id=1, source_target_pairs={{0,24},{4,28},{8,0},{12,4},{16,8},{20,12},{24,16},{28,20},{1,25},{... | collective-permute-start | bytes 196616 | tf_op jit(solution)/shard_map/ppermute | solution.py:34
  107.1 3.5 %collective-permute-start.7 = (f32[1,2,32,256]{3,2,1,0:T(8,128)S(1)}, f32[1,2,32,256]{3,2,1,0:T(8,128)S(1)}, u32[]{:S(2)}, u32[]{:S(2)}) collective-permute-start(f32[1,2,32,256]{3,2,1,0:T(8,128)S(1)} %get-tuple-element.549), channel_id=1, source_target_pairs={{0,28},{4,0},{8,4},{12,8},{16,12},{20,16},{24,20},{28,24},{1,29},{... | collective-permute-start | bytes 196616 | tf_op jit(solution)/shard_map/ppermute | solution.py:34
  108.2 4.7 %collective-permute-start.8 = (f32[1,2,32,256]{3,2,1,0:T(8,128)S(1)}, f32[1,2,32,256]{3,2,1,0:T(8,128)S(1)}, u32[]{:S(2)}, u32[]{:S(2)}) collective-permute-start(f32[1,2,32,256]{3,2,1,0:T(8,128)S(1)} %get-tuple-element.548), channel_id=1, source_target_pairs={{0,4},{4,8},{8,12},{12,16},{16,20},{20,24},{24,28},{28,0},{1,5},{5... | collective-permute-start | bytes 196616 | tf_op jit(solution)/shard_map/ppermute | solution.py:34
  108.2 6.7 %collective-permute-start.9 = (f32[1,2,32,256]{3,2,1,0:T(8,128)S(1)}, f32[1,2,32,256]{3,2,1,0:T(8,128)S(1)}, u32[]{:S(2)}, u32[]{:S(2)}) collective-permute-start(f32[1,2,32,256]{3,2,1,0:T(8,128)S(1)} %get-tuple-element.547), channel_id=1, source_target_pairs={{0,8},{4,12},{8,16},{12,20},{16,24},{20,28},{24,0},{28,4},{1,9},{5... | collective-permute-start | bytes 196616 | tf_op jit(solution)/shard_map/ppermute | solution.py:34
  115.0 5.4 %collective-permute-start.14 = (f32[1,2,32,256]{3,2,1,0:T(8,128)S(1)}, f32[1,2,32,256]{3,2,1,0:T(8,128)S(1)}, u32[]{:S(2)}, u32[]{:S(2)}) collective-permute-start(f32[1,2,32,256]{3,2,1,0:T(8,128)S(1)} %add_divide_fusion.1), channel_id=1, source_target_pairs={{0,8},{4,12},{8,16},{12,20},{16,24},{20,28},{24,0},{28,4},{1,9},{5... | collective-permute-start | bytes 196616 | tf_op jit(solution)/shard_map/ppermute | solution.py:34
  115.0 5.4 %collective-permute-start.15 = (f32[1,2,32,256]{3,2,1,0:T(8,128)S(1)}, f32[1,2,32,256]{3,2,1,0:T(8,128)S(1)}, u32[]{:S(2)}, u32[]{:S(2)}) collective-permute-start(f32[1,2,32,256]{3,2,1,0:T(8,128)S(1)} %add_divide_fusion.1), channel_id=1, source_target_pairs={{0,4},{4,8},{8,12},{12,16},{16,20},{20,24},{24,28},{28,0},{1,5},{5... | collective-permute-start | bytes 196616 | tf_op jit(solution)/shard_map/ppermute | solution.py:34
  115.1 5.3 %collective-permute-start.16 = (f32[1,2,32,256]{3,2,1,0:T(8,128)S(1)}, f32[1,2,32,256]{3,2,1,0:T(8,128)S(1)}, u32[]{:S(2)}, u32[]{:S(2)}) collective-permute-start(f32[1,2,32,256]{3,2,1,0:T(8,128)S(1)} %add_divide_fusion.1), channel_id=1, source_target_pairs={{0,28},{4,0},{8,4},{12,8},{16,12},{20,16},{24,20},{28,24},{1,29},{... | collective-permute-start | bytes 196616 | tf_op jit(solution)/shard_map/ppermute | solution.py:34
  117.7 4.5 %collective-permute-start.17 = (f32[1,2,32,256]{3,2,1,0:T(8,128)S(1)}, f32[1,2,32,256]{3,2,1,0:T(8,128)S(1)}, u32[]{:S(2)}, u32[]{:S(2)}) collective-permute-start(f32[1,2,32,256]{3,2,1,0:T(8,128)S(1)} %add_divide_fusion.1), channel_id=1, source_target_pairs={{0,24},{4,28},{8,0},{12,4},{16,8},{20,12},{24,16},{28,20},{1,25},{... | collective-permute-start | bytes 196616 | tf_op jit(solution)/shard_map/ppermute | solution.py:34
  130.8 4.5 %copy-start.5 = (f32[1,4,128,128]{3,2,1,0:T(8,128)S(1)}, f32[1,4,128,128]{3,2,1,0:T(8,128)}, u32[]{:S(2)}) copy-start(f32[1,4,128,128]{3,2,1,0:T(8,128)} %param.15) | copy-start | bytes 786436
  139.8 2.5 copy-start.8
  171.4 5.1 %collective-permute-start.18 = (f32[1,2,32,256]{3,2,1,0:T(8,128)S(1)}, f32[1,2,32,256]{3,2,1,0:T(8,128)S(1)}, u32[]{:S(2)}, u32[]{:S(2)}) collective-permute-start(f32[1,2,32,256]{3,2,1,0:T(8,128)S(1)} %get-tuple-element.542), channel_id=1, source_target_pairs={{0,24},{4,28},{8,0},{12,4},{16,8},{20,12},{24,16},{28,20},{1,25},{... | collective-permute-start | bytes 196616 | tf_op jit(solution)/shard_map/ppermute | solution.py:34
  174.2 3.7 %collective-permute-start.19 = (f32[1,2,32,256]{3,2,1,0:T(8,128)S(1)}, f32[1,2,32,256]{3,2,1,0:T(8,128)S(1)}, u32[]{:S(2)}, u32[]{:S(2)}) collective-permute-start(f32[1,2,32,256]{3,2,1,0:T(8,128)S(1)} %get-tuple-element.545), channel_id=1, source_target_pairs={{0,28},{4,0},{8,4},{12,8},{16,12},{20,16},{24,20},{28,24},{1,29},{... | collective-permute-start | bytes 196616 | tf_op jit(solution)/shard_map/ppermute | solution.py:34
  174.2 4.6 %collective-permute-start.20 = (f32[1,2,32,256]{3,2,1,0:T(8,128)S(1)}, f32[1,2,32,256]{3,2,1,0:T(8,128)S(1)}, u32[]{:S(2)}, u32[]{:S(2)}) collective-permute-start(f32[1,2,32,256]{3,2,1,0:T(8,128)S(1)} %get-tuple-element.544), channel_id=1, source_target_pairs={{0,4},{4,8},{8,12},{12,16},{16,20},{20,24},{24,28},{28,0},{1,5},{5... | collective-permute-start | bytes 196616 | tf_op jit(solution)/shard_map/ppermute | solution.py:34
  174.7 5.5 %collective-permute-start.21 = (f32[1,2,32,256]{3,2,1,0:T(8,128)S(1)}, f32[1,2,32,256]{3,2,1,0:T(8,128)S(1)}, u32[]{:S(2)}, u32[]{:S(2)}) collective-permute-start(f32[1,2,32,256]{3,2,1,0:T(8,128)S(1)} %get-tuple-element.543), channel_id=1, source_target_pairs={{0,8},{4,12},{8,16},{12,20},{16,24},{20,28},{24,0},{28,4},{1,9},{5... | collective-permute-start | bytes 196616 | tf_op jit(solution)/shard_map/ppermute | solution.py:34
  180.2 5.6 %collective-permute-start.22 = (f32[1,2,32,256]{3,2,1,0:T(8,128)S(1)}, f32[1,2,32,256]{3,2,1,0:T(8,128)S(1)}, u32[]{:S(2)}, u32[]{:S(2)}) collective-permute-start(f32[1,2,32,256]{3,2,1,0:T(8,128)S(1)} %add_divide_fusion), channel_id=1, source_target_pairs={{0,8},{4,12},{8,16},{12,20},{16,24},{20,28},{24,0},{28,4},{1,9},{5... | collective-permute-start | bytes 196616 | tf_op jit(solution)/shard_map/ppermute | solution.py:34
  181.2 5.0 %collective-permute-start.23 = (f32[1,2,32,256]{3,2,1,0:T(8,128)S(1)}, f32[1,2,32,256]{3,2,1,0:T(8,128)S(1)}, u32[]{:S(2)}, u32[]{:S(2)}) collective-permute-start(f32[1,2,32,256]{3,2,1,0:T(8,128)S(1)} %add_divide_fusion), channel_id=1, source_target_pairs={{0,4},{4,8},{8,12},{12,16},{16,20},{20,24},{24,28},{28,0},{1,5},{5... | collective-permute-start | bytes 196616 | tf_op jit(solution)/shard_map/ppermute | solution.py:34
  181.2 5.0 %collective-permute-start.24 = (f32[1,2,32,256]{3,2,1,0:T(8,128)S(1)}, f32[1,2,32,256]{3,2,1,0:T(8,128)S(1)}, u32[]{:S(2)}, u32[]{:S(2)}) collective-permute-start(f32[1,2,32,256]{3,2,1,0:T(8,128)S(1)} %add_divide_fusion), channel_id=1, source_target_pairs={{0,28},{4,0},{8,4},{12,8},{16,12},{20,16},{24,20},{28,24},{1,29},{... | collective-permute-start | bytes 196616 | tf_op jit(solution)/shard_map/ppermute | solution.py:34
  183.8 4.3 %collective-permute-start.25 = (f32[1,2,32,256]{3,2,1,0:T(8,128)S(1)}, f32[1,2,32,256]{3,2,1,0:T(8,128)S(1)}, u32[]{:S(2)}, u32[]{:S(2)}) collective-permute-start(f32[1,2,32,256]{3,2,1,0:T(8,128)S(1)} %add_divide_fusion), channel_id=1, source_target_pairs={{0,24},{4,28},{8,0},{12,4},{16,8},{20,12},{24,16},{28,20},{1,25},{... | collective-permute-start | bytes 196616 | tf_op jit(solution)/shard_map/ppermute | solution.py:34
  197.1 4.5 %copy-start.6 = (f32[1,4,128,128]{3,2,1,0:T(8,128)S(1)}, f32[1,4,128,128]{3,2,1,0:T(8,128)}, u32[]{:S(2)}) copy-start(f32[1,4,128,128]{3,2,1,0:T(8,128)} %param.15) | copy-start | bytes 786436
  237.8 4.5 %collective-permute-start.26 = (f32[1,2,32,256]{3,2,1,0:T(8,128)S(1)}, f32[1,2,32,256]{3,2,1,0:T(8,128)S(1)}, u32[]{:S(2)}, u32[]{:S(2)}) collective-permute-start(f32[1,2,32,256]{3,2,1,0:T(8,128)S(1)} %get-tuple-element.538), channel_id=1, source_target_pairs={{0,24},{4,28},{8,0},{12,4},{16,8},{20,12},{24,16},{28,20},{1,25},{... | collective-permute-start | bytes 196616 | tf_op jit(solution)/shard_map/ppermute | solution.py:34
  239.9 3.7 %collective-permute-start.27 = (f32[1,2,32,256]{3,2,1,0:T(8,128)S(1)}, f32[1,2,32,256]{3,2,1,0:T(8,128)S(1)}, u32[]{:S(2)}, u32[]{:S(2)}) collective-permute-start(f32[1,2,32,256]{3,2,1,0:T(8,128)S(1)} %get-tuple-element.541), channel_id=1, source_target_pairs={{0,28},{4,0},{8,4},{12,8},{16,12},{20,16},{24,20},{28,24},{1,29},{... | collective-permute-start | bytes 196616 | tf_op jit(solution)/shard_map/ppermute | solution.py:34
  239.9 4.6 %collective-permute-start.28 = (f32[1,2,32,256]{3,2,1,0:T(8,128)S(1)}, f32[1,2,32,256]{3,2,1,0:T(8,128)S(1)}, u32[]{:S(2)}, u32[]{:S(2)}) collective-permute-start(f32[1,2,32,256]{3,2,1,0:T(8,128)S(1)} %get-tuple-element.540), channel_id=1, source_target_pairs={{0,4},{4,8},{8,12},{12,16},{16,20},{20,24},{24,28},{28,0},{1,5},{5... | collective-permute-start | bytes 196616 | tf_op jit(solution)/shard_map/ppermute | solution.py:34
  240.4 5.5 %collective-permute-start.29 = (f32[1,2,32,256]{3,2,1,0:T(8,128)S(1)}, f32[1,2,32,256]{3,2,1,0:T(8,128)S(1)}, u32[]{:S(2)}, u32[]{:S(2)}) collective-permute-start(f32[1,2,32,256]{3,2,1,0:T(8,128)S(1)} %get-tuple-element.539), channel_id=1, source_target_pairs={{0,8},{4,12},{8,16},{12,20},{16,24},{20,28},{24,0},{28,4},{1,9},{5... | collective-permute-start | bytes 196616 | tf_op jit(solution)/shard_map/ppermute | solution.py:34
  246.0 4.1 %collective-permute-start.30 = (f32[1,2,8,256]{3,2,1,0:T(8,128)S(1)}, f32[1,2,8,256]{3,2,1,0:T(8,128)S(1)}, u32[]{:S(2)}, u32[]{:S(2)}) collective-permute-start(f32[1,2,8,256]{3,2,1,0:T(8,128)S(1)} %get-tuple-element.556), channel_id=1, source_target_pairs={{0,4},{4,8},{8,12},{12,16},{16,20},{20,24},{24,28},{28,0},{1,5},{5... | collective-permute-start | bytes 49160 | tf_op jit(solution)/shard_map/ppermute | solution.py:23
  246.0 4.1 %collective-permute-start.31 = (f32[1,2,8,256]{3,2,1,0:T(8,128)S(1)}, f32[1,2,8,256]{3,2,1,0:T(8,128)S(1)}, u32[]{:S(2)}, u32[]{:S(2)}) collective-permute-start(f32[1,2,8,256]{3,2,1,0:T(8,128)S(1)} %get-tuple-element.557), channel_id=1, source_target_pairs={{4,0},{8,4},{12,8},{16,12},{20,16},{24,20},{28,24},{0,28},{5,1},{9... | collective-permute-start | bytes 49160 | tf_op jit(solution)/shard_map/ppermute | solution.py:26
where the time goes:
time: 273 us; the launch traced here: 269 us
  local copies, waits for them, and re-layouts  73.2 us (27%)
  loops' own time  66.1 us (24%)
  matrix products  42.3 us (15%)
  waiting for transfers between devices  35.9 us (13%)
  starting transfers between devices  31.4 us (12%)
  blocking collectives  15.1 us (6%)
  other arithmetic  4.05 us (1%)
    another operation x4, loops' own time, deposit(): return lax.fori_loop(0, frame_total, add_one, target)  65.2 us
    ppermute x28, waiting for transfers between devices, passed_along(): return lax.ppermute(value, axis, pairs)  34.5 us
    ppermute x28, starting transfers between devices, passed_along(): return lax.ppermute(value, axis, pairs)  25.4 us
    dynamic_update_slice x16, local copies, waits for them, and re-layouts, add_one(): return lax.dynamic_update_slice(running, current + addition, corner)  25 us
    gather x36, local copies, waits for them, and re-layouts  23.8 us
    dynamic_slice x32, local copies, waits for them, and re-layouts, add_one(): corner = (0,) * leading + (start_cols[frame_index], start_rows[frame_index])  20.8 us
    all_gather x1, blocking collectives, per_device(): every_rim = lax.all_gather(change_rim, 'ang', axis=0, tiled=True)  15.1 us
    ppermute x2, starting transfers between devices, padded_2(): lax.ppermute(lax.slice_in_dim(block, 0, width, axis=dim), axis, backward)  5.5 us
  transfers between devices with their start and end apart: 32, of which 21 were waited for; matrix products, arithmetic and copies ran while one was open for 18% of the time, Pallas kernels for 0%

commit v1 on v0

--- a/solution.py
+++ b/solution.py
@@ -12,6 +12,22 @@
 INTERSECTION_WEIGHT = 1.0
 RELAXATION = 0.5
 HIGHEST = lax.Precision.HIGHEST
+
+
+def ring_product(value, axis, dim, contribution):
+    size, index, span = (lax.axis_size(axis), lax.axis_index(axis), value.shape[dim])
+    forward = [(i, (i + 1) % size) for i in range(size)]
+    left = [(i, (i - 1) % size) for i in range(size)]
+    middle = size // 2
+    from_left = from_right = value
+    total = contribution(value, index * span)
+    for turn in range(1, middle + 1):
+        from_left = lax.ppermute(from_left, axis, forward)
+        if turn < size - middle:
+            from_right = lax.ppermute(from_right, axis, left)
+            total = total + contribution(from_right, (index + turn) % size * span)
+        total = total + contribution(from_left, (index - turn) % size * span)
+    return total
 
 
 def padded_2(block, sides, width):
@@ -165,12 +181,21 @@
         estimate = (numerator + INTERSECTION_WEIGHT * estimate) / (coverage + INTERSECTION_WEIGHT)
     change = estimate - projected
     change_rim = padded_2(change, (("pos", 2),), SH)
-    every_rim = lax.all_gather(change_rim, "ang", axis=0, tiled=True)
     back_pick = (
         padded_cols[None, None, None, :]
         == columns[None, None, :, None] + SH - shear_steps[:, :, None, None]
     ).astype(jnp.float32)
-    accumulated = jnp.einsum("azxk,acky->czxy", back_pick, every_rim, precision=HIGHEST)
+    accumulated = ring_product(
+        change_rim,
+        "ang",
+        0,
+        lambda own_block, offset_2: jnp.einsum(
+            "azxk,acky->czxy",
+            lax.dynamic_slice_in_dim(back_pick, offset_2, own_block.shape[0], axis=0),
+            own_block,
+            precision=HIGHEST,
+        ),
+    )
     return object_field + RELAXATION / shear_steps.shape[0] * accumulated
 
 

time: 273 us -> 278 us (1.018)
  waiting for transfers between devices: 35.9 us -> 51.4 us
  blocking collectives: 15.1 us -> 0 us
  starting transfers between devices: 31.4 us -> 37.4 us
  loops' own time: 66.1 us -> 62.1 us
    all_gather x1 -> x0, blocking collectives: 15.1 us -> none  [per_device(): every_rim = lax.all_gather(change_rim, 'ang', axis=0, tiled=True)]
    ppermute x2, waiting for transfers between devices: 1.32 us -> 11.1 us  [padded_2(): lax.ppermute(lax.slice_in_dim(block, block.shape[dim] - width, None, axis...]
    ppermute x0 -> x3, waiting for transfers between devices: none -> 9.28 us  [the longest x2 9.28 us: ring_product(): from_left = lax.ppermute(from_left, axis, forward)]
    ppermute x0 -> x3, starting transfers between devices: none -> 4.25 us  [the longest x1 3.66 us: ring_product(): from_right = lax.ppermute(from_right, axis, left)]
    ppermute x28, waiting for transfers between devices: 34.5 us -> 30.3 us  [passed_along(): return lax.ppermute(value, axis, pairs)]
    another operation x4, loops' own time: 65.2 us -> 61.5 us  [deposit(): return lax.fori_loop(0, frame_total, add_one, target)]
    dot_general x1 -> x4, matrix products: 3.62 us -> 5.75 us  [per_device(): jnp.einsum('azxk,acky->czxy', lax.dynamic_slice_in_dim(back_pick, offset_...]
  transfers between devices with their start and end apart: 32 -> 35, of which waited for: 21 -> 19; matrix products, arithmetic and copies ran while one was open for 18% -> 15% of each run, Pallas kernels for 0% -> 0%
where the time goes in v1:
time: 278 us; the launch traced here: 274 us
  local copies, waits for them, and re-layouts  72.8 us (26%)
  loops' own time  62.1 us (22%)
  waiting for transfers between devices  51.4 us (18%)
  matrix products  44.6 us (16%)
  starting transfers between devices  37.4 us (13%)
  other arithmetic  4.71 us (2%)
    another operation x4, loops' own time, deposit(): return lax.fori_loop(0, frame_total, add_one, target)  61.5 us
    ppermute x28, waiting for transfers between devices, passed_along(): return lax.ppermute(value, axis, pairs)  30.3 us
    ppermute x28, starting transfers between devices, passed_along(): return lax.ppermute(value, axis, pairs)  27.8 us
    dynamic_update_slice x16, local copies, waits for them, and re-layouts, add_one(): return lax.dynamic_update_slice(running, current + addition, corner)  25 us
    gather x36, local copies, waits for them, and re-layouts  24 us
    dynamic_slice x32, local copies, waits for them, and re-layouts, add_one(): corner = (0,) * leading + (start_cols[frame_index], start_rows[frame_index])  19.6 us
    ppermute x2, waiting for transfers between devices, padded_2(): lax.ppermute(lax.slice_in_dim(block, block.shape[dim] - width, None, axis...  11.1 us
    ppermute x2, waiting for transfers between devices, ring_product(): from_left = lax.ppermute(from_left, axis, forward)  9.28 us
  transfers between devices with their start and end apart: 35, of which 19 were waited for; matrix products, arithmetic and copies ran while one was open for 15% of the time, Pallas kernels for 0%

profile of v1, /device:TPU:0, one launch (start us, length us, event | category | flops | bytes accessed | tf_op | source)
XLA Modules:
  0.0 274.0 jit_solution(14299085803101776814)
XLA Ops:
  1.9 26.2 %while.56 = (s32[]{:T(128)}, f32[160,256]{1,0:T(8,128)S(1)}, s32[4]{0:T(128)S(1)}, s32[4]{0:T(128)S(1)}, f32[128,128]{1,0:T(8,128)S(1)}, /*index=5*/s32[]{:T(128)}, s32[]{:T(128)}, s32[]{:T(128)}, s32[]{:T(128)}) while((s32[]{:T(128)}, f32[160,256]{1,0:T(8,128)S(1)}, s32[4]{0:T(128)S(1)}, s32[4]{0:T(128)S(1)}, f32[128,128]{1,0:T(8,128)S(1)}, ...), condition=%wide.region_3.4_spmd, body=%wide.region_2.3_spmd.sunk | while | flops 16392 | bytes 327885 | solution.py:87
  13.3 1.1 dynamic_update_slice.33
  19.6 1.7 dynamic_update_slice.33
  26.4 1.7 dynamic_update_slice.33
  28.8 4.0 %collective-permute-start.10 = (f32[32,256]{1,0:T(8,128)}, f32[32,256]{1,0:T(8,128)S(1)}, u32[]{:S(2)}, u32[]{:S(2)}) collective-permute-start(f32[32,256]{1,0:T(8,128)} %get-tuple-element.535), channel_id=1, source_target_pairs={{0,24},{4,28},{8,0},{12,4},{16,8},{20,12},{24,16},{28,20},{1,25},{... | collective-permute-start | bytes 98312 | tf_op jit(solution)/shard_map/ppermute | solution.py:50
  32.8 2.1 fusion.393
  34.9 2.1 collective-permute-start
  37.8 10.5 %collective-permute-done = f32[2,32,8,256]{3,2,1,0:T(8,128)} collective-permute-done((f32[2,32,8,256]{3,2,1,0:T(8,128)}, f32[2,32,8,256]{3,2,1,0:T(8,128)}, u32[]{:S(2)}, u32[]{:S(2)}) %collective-permute-start) | collective-permute-done | bytes 524320 | tf_op jit(solution)/shard_map/ppermute | solution.py:39
  48.9 2.5 fusion.30
  51.4 1.6 collective-permute-start.2
  53.1 4.2 %collective-permute-done.2 = f32[1,2,32,256]{3,2,1,0:T(8,128)S(1)} collective-permute-done((f32[1,2,32,256]{3,2,1,0:T(8,128)S(1)}, f32[1,2,32,256]{3,2,1,0:T(8,128)S(1)}, u32[]{:S(2)}, u32[]{:S(2)}) %collective-permute-start.2) | collective-permute-done | bytes 65568 | tf_op jit(solution)/shard_map/ppermute | solution.py:50
  57.4 4.5 %collective-permute-done.3 = f32[1,2,32,256]{3,2,1,0:T(8,128)S(1)} collective-permute-done((f32[1,2,32,256]{3,2,1,0:T(8,128)S(1)}, f32[1,2,32,256]{3,2,1,0:T(8,128)S(1)}, u32[]{:S(2)}, u32[]{:S(2)}) %collective-permute-start.3) | collective-permute-done | bytes 65568 | tf_op jit(solution)/shard_map/ppermute | solution.py:50
  61.9 1.9 collective-permute-done.4
  64.5 4.1 %collective-permute-done.5 = f32[1,2,32,256]{3,2,1,0:T(8,128)S(1)} collective-permute-done((f32[1,2,32,256]{3,2,1,0:T(8,128)S(1)}, f32[1,2,32,256]{3,2,1,0:T(8,128)S(1)}, u32[]{:S(2)}, u32[]{:S(2)}) %collective-permute-start.5) | collective-permute-done | bytes 65568 | tf_op jit(solution)/shard_map/ppermute | solution.py:50
  68.6 8.4 %while.59 = (s32[]{:T(128)}, f32[1,2,160,256]{3,2,1,0:T(8,128)S(1)}, s32[4,4]{1,0:T(4,128)S(1)}, f32[4,1,2,128,128]{4,3,0,2,1:T(8,128)S(1)}, s32[]{:T(128)}) while((s32[]{:T(128)}, f32[1,2,160,256]{3,2,1,0:T(8,128)S(1)}, s32[4,4]{1,0:T(4,128)S(1)}, f32[4,1,2,128,128]{4,3,0,2,1:T(8,128)S(1)}, s32[]{:T(128)}) %tuple.169), condition=%wide.while_cond, body=%wide.while_body.sunk | while | flops 2 | bytes 262277 | solution.py:94
  69.3 1.4 bitcast_dynamic-update-slice_fusion.6
  71.4 1.4 bitcast_dynamic-update-slice_fusion.6
  73.4 1.4 bitcast_dynamic-update-slice_fusion.6
  75.5 1.4 bitcast_dynamic-update-slice_fusion.6
  88.3 1.1 add_bitcast_fusion.2
  89.5 27.2 %while.55 = (s32[]{:T(128)}, f32[1,2,160,256]{3,2,1,0:T(8,128)S(1)}, s32[4]{0:T(128)S(1)}, s32[4]{0:T(128)S(1)}, f32[1,2,4,128,128]{4,3,2,1,0:T(8,128)S(1)}, /*index=5*/s32[]{:T(128)}, s32[]{:T(128)}, s32[]{:T(128)}, s32[]{:T(128)}) while((s32[]{:T(128)}, f32[1,2,160,256]{3,2,1,0:T(8,128)S(1)}, s32[4]{0:T(128)S(1)}, s32[4]{0:T(128)S(1)}, ...), condition=%wide.region_1.2_spmd, body=%wide.region_0.1_spmd.sunk | while | flops 32776 | bytes 655569 | solution.py:87
  100.9 1.2 dynamic_update_slice.32
  107.3 2.1 dynamic_update_slice.32
  114.6 2.1 dynamic_update_slice.32
  116.8 1.2 collective-permute-start.6
  118.9 2.6 collective-permute-start.7
  122.3 1.5 collective-permute-done.9
  125.1 2.3 collective-permute-start.17
  127.9 2.4 collective-permute-done.14
  130.3 2.1 collective-permute-done.15
  132.5 8.0 %while.60 = (s32[]{:T(128)}, f32[1,2,160,256]{3,2,1,0:T(8,128)S(1)}, s32[4,4]{1,0:T(4,128)S(1)}, f32[4,1,2,128,128]{4,3,0,2,1:T(8,128)S(1)}, s32[]{:T(128)}) while((s32[]{:T(128)}, f32[1,2,160,256]{3,2,1,0:T(8,128)S(1)}, s32[4,4]{1,0:T(4,128)S(1)}, f32[4,1,2,128,128]{4,3,0,2,1:T(8,128)S(1)}, s32[]{:T(128)}) %tuple.190), condition=%wide.while_cond.1, body=%wide.while_body.1.sunk | while | flops 2 | bytes 262277 | solution.py:94
  133.2 1.3 bitcast_dynamic-update-slice_fusion.7
  135.2 1.3 bitcast_dynamic-update-slice_fusion.7
  137.2 1.3 bitcast_dynamic-update-slice_fusion.7
  139.2 1.3 bitcast_dynamic-update-slice_fusion.7
  152.7 27.2 %while.57 = (s32[]{:T(128)}, f32[1,2,160,256]{3,2,1,0:T(8,128)S(1)}, s32[4]{0:T(128)S(1)}, s32[4]{0:T(128)S(1)}, f32[1,2,4,128,128]{4,3,2,1,0:T(8,128)S(1)}, /*index=5*/s32[]{:T(128)}, s32[]{:T(128)}, s32[]{:T(128)}, s32[]{:T(128)}) while((s32[]{:T(128)}, f32[1,2,160,256]{3,2,1,0:T(8,128)S(1)}, s32[4]{0:T(128)S(1)}, s32[4]{0:T(128)S(1)}, ...), condition=%wide.region_5.6_spmd, body=%wide.region_4.5_spmd.sunk | while | flops 32776 | bytes 655569 | solution.py:87
  157.9 1.0 dynamic_update_slice.34
  164.1 1.2 dynamic_update_slice.34
  170.5 2.1 dynamic_update_slice.34
  177.8 2.1 dynamic_update_slice.34
  180.0 1.2 collective-permute-start.18
  182.1 2.6 collective-permute-start.19
  184.7 2.1 collective-permute-done.21
  187.5 2.7 collective-permute-start.25
  190.9 1.8 collective-permute-done.22
  192.7 2.7 collective-permute-done.23
  195.6 8.2 %while.61 = (s32[]{:T(128)}, f32[1,2,160,256]{3,2,1,0:T(8,128)S(1)}, s32[4,4]{1,0:T(4,128)S(1)}, f32[4,1,2,128,128]{4,3,0,2,1:T(8,128)S(1)}, s32[]{:T(128)}) while((s32[]{:T(128)}, f32[1,2,160,256]{3,2,1,0:T(8,128)S(1)}, s32[4,4]{1,0:T(4,128)S(1)}, f32[4,1,2,128,128]{4,3,0,2,1:T(8,128)S(1)}, s32[]{:T(128)}) %tuple.191), condition=%wide.while_cond.2, body=%wide.while_body.2.sunk | while | flops 2 | bytes 262277 | solution.py:94
  196.3 1.4 bitcast_dynamic-update-slice_fusion.8
  198.3 1.4 bitcast_dynamic-update-slice_fusion.8
  200.4 1.4 bitcast_dynamic-update-slice_fusion.8
  202.4 1.4 bitcast_dynamic-update-slice_fusion.8
  216.1 27.2 %while.58 = (s32[]{:T(128)}, f32[1,2,160,256]{3,2,1,0:T(8,128)S(1)}, s32[4]{0:T(128)S(1)}, s32[4]{0:T(128)S(1)}, f32[1,2,4,128,128]{4,3,2,1,0:T(8,128)S(1)}, /*index=5*/s32[]{:T(128)}, s32[]{:T(128)}, s32[]{:T(128)}, s32[]{:T(128)}) while((s32[]{:T(128)}, f32[1,2,160,256]{3,2,1,0:T(8,128)S(1)}, s32[4]{0:T(128)S(1)}, s32[4]{0:T(128)S(1)}, ...), condition=%wide.region_7.8_spmd, body=%wide.region_6.7_spmd.sunk | while | flops 32776 | bytes 655569 | solution.py:87
  221.3 1.0 dynamic_update_slice.35
  227.5 1.2 dynamic_update_slice.35
  233.9 2.1 dynamic_update_slice.35
  241.2 2.1 dynamic_update_slice.35
  243.4 1.0 collective-permute-start.26
  245.5 2.6 collective-permute-start.27
  248.2 1.6 collective-permute-done.29
  250.7 2.3 collective-permute-start.31
  254.5 3.7 %collective-permute-start.32 = (f32[1,2,48,256]{3,2,1,0:T(8,128)S(1)}, f32[1,2,48,256]{3,2,1,0:T(8,128)S(1)}, u32[]{:S(2)}, u32[]{:S(2)}) collective-permute-start(f32[1,2,48,256]{3,2,1,0:T(8,128)S(1)} %pad_maximum_fusion.3), channel_id=1, source_target_pairs={{0,3},{1,0},{2,1},{3,2},{4,7},{5,4},{6,5},{7,6},{8,11},{9,8},{10,9... | collective-permute-start | bytes 294920 | tf_op jit(solution)/shard_map/ppermute | solution.py:27
  259.1 5.4 %collective-permute-done.33 = f32[1,2,48,256]{3,2,1,0:T(8,128)S(1)} collective-permute-done((f32[1,2,48,256]{3,2,1,0:T(8,128)S(1)}, f32[1,2,48,256]{3,2,1,0:T(8,128)S(1)}, u32[]{:S(2)}, u32[]{:S(2)}) %collective-permute-start.33) | collective-permute-done | bytes 98336 | tf_op jit(solution)/shard_map/ppermute | solution.py:25
  267.1 3.8 %collective-permute-done.34 = f32[1,2,48,256]{3,2,1,0:T(8,128)S(1)} collective-permute-done((f32[1,2,48,256]{3,2,1,0:T(8,128)S(1)}, f32[1,2,48,256]{3,2,1,0:T(8,128)S(1)}, u32[]{:S(2)}, u32[]{:S(2)}) %collective-permute-start.34) | collective-permute-done | bytes 98336 | tf_op jit(solution)/shard_map/ppermute | solution.py:25
  271.0 2.8 %bitcast_add_fusion.3 = f32[2,32,32,256]{3,2,1,0:T(8,128)} fusion(f32[2,32,32,256]{3,2,1,0:T(8,128)S(1)} %copy-done, f32[2,256,32,32]{1,3,2,0:T(8,128)S(1)} %fusion.36, f32[2,256,32,32]{1,3,2,0:T(8,128)S(1)} %fusion.40, f32[2,256,32,32]{1,3,2,0:T(8,128)S(1)} %fusion.38, pred[4,32,32,48]{3,2,1,0:T(32,128)(4,1)S(1)} %iota_compare_fusion, s32[]{:T(128)S(6)} %select_n.251, ...), kind=kOutput, calls=%fused_computation.16 | convolution fusion | flops 304611328 | bytes 10715140 | tf_op jit(solution)/shard_map/azxk,acky->czxy/dot_general | solution.py:192
  (234 shorter events, 84.4 us)
Async XLA Ops:
  1.9 35.8 %copy-start.2 = (s32[4,32]{1,0:T(4,128)S(1)}, s32[4,32]{1,0:T(4,128)}, u32[]{:S(2)}) copy-start(s32[4,32]{1,0:T(4,128)} %param.17) | copy-start | bytes 1540
  1.9 35.9 %copy-start.1 = (f32[2,128,128]{2,1,0:T(8,128)S(1)}, f32[2,128,128]{2,1,0:T(8,128)}, u32[]{:S(2)}) copy-start(f32[2,128,128]{2,1,0:T(8,128)} %param.14) | copy-start | bytes 393220
  1.9 46.9 %copy-start = (f32[2,32,32,256]{3,2,1,0:T(8,128)S(1)}, f32[2,32,32,256]{3,2,1,0:T(8,128)}, u32[]{:S(2)}) copy-start(f32[2,32,32,256]{3,2,1,0:T(8,128)} %param.13) | copy-start | bytes 6291460
  28.8 89.2 %collective-permute-start.10 = (f32[32,256]{1,0:T(8,128)}, f32[32,256]{1,0:T(8,128)S(1)}, u32[]{:S(2)}, u32[]{:S(2)}) collective-permute-start(f32[32,256]{1,0:T(8,128)} %get-tuple-element.535), channel_id=1, source_target_pairs={{0,24},{4,28},{8,0},{12,4},{16,8},{20,12},{24,16},{28,20},{1,25},{... | collective-permute-start | bytes 98312 | tf_op jit(solution)/shard_map/ppermute | solution.py:50
  32.8 86.0 %collective-permute-start.13 = (f32[32,256]{1,0:T(8,128)}, f32[32,256]{1,0:T(8,128)S(1)}, u32[]{:S(2)}, u32[]{:S(2)}) collective-permute-start(f32[32,256]{1,0:T(8,128)} %get-tuple-element.536), channel_id=1, source_target_pairs={{0,8},{4,12},{8,16},{12,20},{16,24},{20,28},{24,0},{28,4},{1,9},{5... | collective-permute-start | bytes 98312 | tf_op jit(solution)/shard_map/ppermute | solution.py:50
  32.8 86.0 %collective-permute-start.12 = (f32[32,256]{1,0:T(8,128)}, f32[32,256]{1,0:T(8,128)}, u32[]{:S(2)}, u32[]{:S(2)}) collective-permute-start(f32[32,256]{1,0:T(8,128)} %get-tuple-element.537), channel_id=1, source_target_pairs={{0,4},{4,8},{8,12},{12,16},{16,20},{20,24},{24,28},{28,0},{1,5},{5... | collective-permute-start | bytes 98312 | tf_op jit(solution)/shard_map/ppermute | solution.py:50
  34.9 13.3 %collective-permute-start = (f32[2,32,8,256]{3,2,1,0:T(8,128)}, f32[2,32,8,256]{3,2,1,0:T(8,128)}, u32[]{:S(2)}, u32[]{:S(2)}) collective-permute-start(f32[2,32,8,256]{3,2,1,0:T(8,128)} %get-tuple-element.509), channel_id=1, source_target_pairs={{0,4},{4,8},{8,12},{12,16},{16,20},{20,24},{24,28},{28,0},{1,5},{5... | collective-permute-start | bytes 1572872 | tf_op jit(solution)/shard_map/ppermute | solution.py:39
  37.0 11.8 %collective-permute-start.1 = (f32[2,32,8,256]{3,2,1,0:T(8,128)S(1)}, f32[2,32,8,256]{3,2,1,0:T(8,128)}, u32[]{:S(2)}, u32[]{:S(2)}) collective-permute-start(f32[2,32,8,256]{3,2,1,0:T(8,128)S(1)} %get-tuple-element.510), channel_id=1, source_target_pairs={{4,0},{8,4},{12,8},{16,12},{20,16},{24,20},{28,24},{0,28},{5,1},{9... | collective-permute-start | bytes 1572872 | tf_op jit(solution)/shard_map/ppermute | solution.py:42
  48.3 73.3 %collective-permute-start.11 = (f32[32,256]{1,0:T(8,128)}, f32[32,256]{1,0:T(8,128)}, u32[]{:S(2)}, u32[]{:S(2)}) collective-permute-start(f32[32,256]{1,0:T(8,128)} %get-tuple-element.538), channel_id=1, source_target_pairs={{0,28},{4,0},{8,4},{12,8},{16,12},{20,16},{24,20},{28,24},{1,29},{... | collective-permute-start | bytes 98312 | tf_op jit(solution)/shard_map/ppermute | solution.py:50
  51.4 5.9 %collective-permute-start.2 = (f32[1,2,32,256]{3,2,1,0:T(8,128)S(1)}, f32[1,2,32,256]{3,2,1,0:T(8,128)S(1)}, u32[]{:S(2)}, u32[]{:S(2)}) collective-permute-start(f32[1,2,32,256]{3,2,1,0:T(8,128)S(1)} %fusion.30), channel_id=1, source_target_pairs={{0,8},{4,12},{8,16},{12,20},{16,24},{20,28},{24,0},{28,4},{1,9},{5... | collective-permute-start | bytes 196616 | tf_op jit(solution)/shard_map/ppermute | solution.py:50
  57.3 4.6 %collective-permute-start.3 = (f32[1,2,32,256]{3,2,1,0:T(8,128)S(1)}, f32[1,2,32,256]{3,2,1,0:T(8,128)S(1)}, u32[]{:S(2)}, u32[]{:S(2)}) collective-permute-start(f32[1,2,32,256]{3,2,1,0:T(8,128)S(1)} %fusion.30), channel_id=1, source_target_pairs={{0,4},{4,8},{8,12},{12,16},{16,20},{20,24},{24,28},{28,0},{1,5},{5... | collective-permute-start | bytes 196616 | tf_op jit(solution)/shard_map/ppermute | solution.py:50
  61.9 1.9 collective-permute-start.4
  63.8 4.8 %collective-permute-start.5 = (f32[1,2,32,256]{3,2,1,0:T(8,128)S(1)}, f32[1,2,32,256]{3,2,1,0:T(8,128)S(1)}, u32[]{:S(2)}, u32[]{:S(2)}) collective-permute-start(f32[1,2,32,256]{3,2,1,0:T(8,128)S(1)} %fusion.30), channel_id=1, source_target_pairs={{0,24},{4,28},{8,0},{12,4},{16,8},{20,12},{24,16},{28,20},{1,25},{... | collective-permute-start | bytes 196616 | tf_op jit(solution)/shard_map/ppermute | solution.py:50
  77.8 4.5 %copy-start.3 = (f32[1,4,128,128]{3,2,1,0:T(8,128)S(1)}, f32[1,4,128,128]{3,2,1,0:T(8,128)}, u32[]{:S(2)}) copy-start(f32[1,4,128,128]{3,2,1,0:T(8,128)} %param.15) | copy-start | bytes 786436
  116.8 4.8 %copy-start.6 = (s32[4]{0:T(128)}, s32[4]{0:T(128)S(1)}, u32[]{:S(2)}) copy-start(s32[4]{0:T(128)S(1)} %get-tuple-element.979) | copy-start | bytes 52
  116.8 5.5 %collective-permute-start.6 = (f32[1,2,32,256]{3,2,1,0:T(8,128)S(1)}, f32[1,2,32,256]{3,2,1,0:T(8,128)S(1)}, u32[]{:S(2)}, u32[]{:S(2)}) collective-permute-start(f32[1,2,32,256]{3,2,1,0:T(8,128)S(1)} %get-tuple-element.531), channel_id=1, source_target_pairs={{0,24},{4,28},{8,0},{12,4},{16,8},{20,12},{24,16},{28,20},{1,25},{... | collective-permute-start | bytes 196616 | tf_op jit(solution)/shard_map/ppermute | solution.py:50
  118.0 5.9 %collective-permute-start.9 = (f32[1,2,32,256]{3,2,1,0:T(8,128)S(1)}, f32[1,2,32,256]{3,2,1,0:T(8,128)S(1)}, u32[]{:S(2)}, u32[]{:S(2)}) collective-permute-start(f32[1,2,32,256]{3,2,1,0:T(8,128)S(1)} %get-tuple-element.532), channel_id=1, source_target_pairs={{0,8},{4,12},{8,16},{12,20},{16,24},{20,28},{24,0},{28,4},{1,9},{5... | collective-permute-start | bytes 196616 | tf_op jit(solution)/shard_map/ppermute | solution.py:50
  118.9 5.5 %collective-permute-start.8 = (f32[1,2,32,256]{3,2,1,0:T(8,128)S(1)}, f32[1,2,32,256]{3,2,1,0:T(8,128)S(1)}, u32[]{:S(2)}, u32[]{:S(2)}) collective-permute-start(f32[1,2,32,256]{3,2,1,0:T(8,128)S(1)} %get-tuple-element.533), channel_id=1, source_target_pairs={{0,4},{4,8},{8,12},{12,16},{16,20},{20,24},{24,28},{28,0},{1,5},{5... | collective-permute-start | bytes 196616 | tf_op jit(solution)/shard_map/ppermute | solution.py:50
  118.9 5.5 %collective-permute-start.7 = (f32[1,2,32,256]{3,2,1,0:T(8,128)S(1)}, f32[1,2,32,256]{3,2,1,0:T(8,128)S(1)}, u32[]{:S(2)}, u32[]{:S(2)}) collective-permute-start(f32[1,2,32,256]{3,2,1,0:T(8,128)S(1)} %get-tuple-element.534), channel_id=1, source_target_pairs={{0,28},{4,0},{8,4},{12,8},{16,12},{20,16},{24,20},{28,24},{1,29},{... | collective-permute-start | bytes 196616 | tf_op jit(solution)/shard_map/ppermute | solution.py:50
  124.5 5.9 %collective-permute-start.14 = (f32[1,2,32,256]{3,2,1,0:T(8,128)S(1)}, f32[1,2,32,256]{3,2,1,0:T(8,128)S(1)}, u32[]{:S(2)}, u32[]{:S(2)}) collective-permute-start(f32[1,2,32,256]{3,2,1,0:T(8,128)S(1)} %add_divide_fusion.1), channel_id=1, source_target_pairs={{0,8},{4,12},{8,16},{12,20},{16,24},{20,28},{24,0},{28,4},{1,9},{5... | collective-permute-start | bytes 196616 | tf_op jit(solution)/shard_map/ppermute | solution.py:50
  125.1 7.3 %collective-permute-start.17 = (f32[1,2,32,256]{3,2,1,0:T(8,128)S(1)}, f32[1,2,32,256]{3,2,1,0:T(8,128)S(1)}, u32[]{:S(2)}, u32[]{:S(2)}) collective-permute-start(f32[1,2,32,256]{3,2,1,0:T(8,128)S(1)} %add_divide_fusion.1), channel_id=1, source_target_pairs={{0,24},{4,28},{8,0},{12,4},{16,8},{20,12},{24,16},{28,20},{1,25},{... | collective-permute-start | bytes 196616 | tf_op jit(solution)/shard_map/ppermute | solution.py:50
  127.4 5.0 %collective-permute-start.16 = (f32[1,2,32,256]{3,2,1,0:T(8,128)S(1)}, f32[1,2,32,256]{3,2,1,0:T(8,128)S(1)}, u32[]{:S(2)}, u32[]{:S(2)}) collective-permute-start(f32[1,2,32,256]{3,2,1,0:T(8,128)S(1)} %add_divide_fusion.1), channel_id=1, source_target_pairs={{0,28},{4,0},{8,4},{12,8},{16,12},{20,16},{24,20},{28,24},{1,29},{... | collective-permute-start | bytes 196616 | tf_op jit(solution)/shard_map/ppermute | solution.py:50
  127.7 4.8 %collective-permute-start.15 = (f32[1,2,32,256]{3,2,1,0:T(8,128)S(1)}, f32[1,2,32,256]{3,2,1,0:T(8,128)S(1)}, u32[]{:S(2)}, u32[]{:S(2)}) collective-permute-start(f32[1,2,32,256]{3,2,1,0:T(8,128)S(1)} %add_divide_fusion.1), channel_id=1, source_target_pairs={{0,4},{4,8},{8,12},{12,16},{16,20},{20,24},{24,28},{28,0},{1,5},{5... | collective-permute-start | bytes 196616 | tf_op jit(solution)/shard_map/ppermute | solution.py:50
  141.3 4.5 %copy-start.4 = (f32[1,4,128,128]{3,2,1,0:T(8,128)S(1)}, f32[1,4,128,128]{3,2,1,0:T(8,128)}, u32[]{:S(2)}) copy-start(f32[1,4,128,128]{3,2,1,0:T(8,128)} %param.15) | copy-start | bytes 786436
  150.3 2.5 copy-start.7
  180.0 4.7 %collective-permute-start.18 = (f32[1,2,32,256]{3,2,1,0:T(8,128)S(1)}, f32[1,2,32,256]{3,2,1,0:T(8,128)S(1)}, u32[]{:S(2)}, u32[]{:S(2)}) collective-permute-start(f32[1,2,32,256]{3,2,1,0:T(8,128)S(1)} %get-tuple-element.527), channel_id=1, source_target_pairs={{0,24},{4,28},{8,0},{12,4},{16,8},{20,12},{24,16},{28,20},{1,25},{... | collective-permute-start | bytes 196616 | tf_op jit(solution)/shard_map/ppermute | solution.py:50
  181.3 5.6 %collective-permute-start.21 = (f32[1,2,32,256]{3,2,1,0:T(8,128)S(1)}, f32[1,2,32,256]{3,2,1,0:T(8,128)S(1)}, u32[]{:S(2)}, u32[]{:S(2)}) collective-permute-start(f32[1,2,32,256]{3,2,1,0:T(8,128)S(1)} %get-tuple-element.528), channel_id=1, source_target_pairs={{0,8},{4,12},{8,16},{12,20},{16,24},{20,28},{24,0},{28,4},{1,9},{5... | collective-permute-start | bytes 196616 | tf_op jit(solution)/shard_map/ppermute | solution.py:50
  182.1 5.0 %collective-permute-start.20 = (f32[1,2,32,256]{3,2,1,0:T(8,128)S(1)}, f32[1,2,32,256]{3,2,1,0:T(8,128)S(1)}, u32[]{:S(2)}, u32[]{:S(2)}) collective-permute-start(f32[1,2,32,256]{3,2,1,0:T(8,128)S(1)} %get-tuple-element.529), channel_id=1, source_target_pairs={{0,4},{4,8},{8,12},{12,16},{16,20},{20,24},{24,28},{28,0},{1,5},{5... | collective-permute-start | bytes 196616 | tf_op jit(solution)/shard_map/ppermute | solution.py:50
  182.1 5.0 %collective-permute-start.19 = (f32[1,2,32,256]{3,2,1,0:T(8,128)S(1)}, f32[1,2,32,256]{3,2,1,0:T(8,128)S(1)}, u32[]{:S(2)}, u32[]{:S(2)}) collective-permute-start(f32[1,2,32,256]{3,2,1,0:T(8,128)S(1)} %get-tuple-element.530), channel_id=1, source_target_pairs={{0,28},{4,0},{8,4},{12,8},{16,12},{20,16},{24,20},{28,24},{1,29},{... | collective-permute-start | bytes 196616 | tf_op jit(solution)/shard_map/ppermute | solution.py:50
  187.2 5.6 %collective-permute-start.22 = (f32[1,2,32,256]{3,2,1,0:T(8,128)S(1)}, f32[1,2,32,256]{3,2,1,0:T(8,128)S(1)}, u32[]{:S(2)}, u32[]{:S(2)}) collective-permute-start(f32[1,2,32,256]{3,2,1,0:T(8,128)S(1)} %add_divide_fusion), channel_id=1, source_target_pairs={{0,8},{4,12},{8,16},{12,20},{16,24},{20,28},{24,0},{28,4},{1,9},{5... | collective-permute-start | bytes 196616 | tf_op jit(solution)/shard_map/ppermute | solution.py:50
  187.5 8.0 %collective-permute-start.25 = (f32[1,2,32,256]{3,2,1,0:T(8,128)S(1)}, f32[1,2,32,256]{3,2,1,0:T(8,128)S(1)}, u32[]{:S(2)}, u32[]{:S(2)}) collective-permute-start(f32[1,2,32,256]{3,2,1,0:T(8,128)S(1)} %add_divide_fusion), channel_id=1, source_target_pairs={{0,24},{4,28},{8,0},{12,4},{16,8},{20,12},{24,16},{28,20},{1,25},{... | collective-permute-start | bytes 196616 | tf_op jit(solution)/shard_map/ppermute | solution.py:50
  190.1 5.4 %collective-permute-start.24 = (f32[1,2,32,256]{3,2,1,0:T(8,128)S(1)}, f32[1,2,32,256]{3,2,1,0:T(8,128)S(1)}, u32[]{:S(2)}, u32[]{:S(2)}) collective-permute-start(f32[1,2,32,256]{3,2,1,0:T(8,128)S(1)} %add_divide_fusion), channel_id=1, source_target_pairs={{0,28},{4,0},{8,4},{12,8},{16,12},{20,16},{24,20},{28,24},{1,29},{... | collective-permute-start | bytes 196616 | tf_op jit(solution)/shard_map/ppermute | solution.py:50
  190.9 4.6 %collective-permute-start.23 = (f32[1,2,32,256]{3,2,1,0:T(8,128)S(1)}, f32[1,2,32,256]{3,2,1,0:T(8,128)S(1)}, u32[]{:S(2)}, u32[]{:S(2)}) collective-permute-start(f32[1,2,32,256]{3,2,1,0:T(8,128)S(1)} %add_divide_fusion), channel_id=1, source_target_pairs={{0,4},{4,8},{8,12},{12,16},{16,20},{20,24},{24,28},{28,0},{1,5},{5... | collective-permute-start | bytes 196616 | tf_op jit(solution)/shard_map/ppermute | solution.py:50
  204.6 4.5 %copy-start.5 = (f32[1,4,128,128]{3,2,1,0:T(8,128)S(1)}, f32[1,4,128,128]{3,2,1,0:T(8,128)}, u32[]{:S(2)}) copy-start(f32[1,4,128,128]{3,2,1,0:T(8,128)} %param.15) | copy-start | bytes 786436
  243.4 4.8 %collective-permute-start.26 = (f32[1,2,32,256]{3,2,1,0:T(8,128)S(1)}, f32[1,2,32,256]{3,2,1,0:T(8,128)S(1)}, u32[]{:S(2)}, u32[]{:S(2)}) collective-permute-start(f32[1,2,32,256]{3,2,1,0:T(8,128)S(1)} %get-tuple-element.523), channel_id=1, source_target_pairs={{0,24},{4,28},{8,0},{12,4},{16,8},{20,12},{24,16},{28,20},{1,25},{... | collective-permute-start | bytes 196616 | tf_op jit(solution)/shard_map/ppermute | solution.py:50
  244.4 5.4 %collective-permute-start.29 = (f32[1,2,32,256]{3,2,1,0:T(8,128)S(1)}, f32[1,2,32,256]{3,2,1,0:T(8,128)S(1)}, u32[]{:S(2)}, u32[]{:S(2)}) collective-permute-start(f32[1,2,32,256]{3,2,1,0:T(8,128)S(1)} %get-tuple-element.524), channel_id=1, source_target_pairs={{0,8},{4,12},{8,16},{12,20},{16,24},{20,28},{24,0},{28,4},{1,9},{5... | collective-permute-start | bytes 196616 | tf_op jit(solution)/shard_map/ppermute | solution.py:50
  245.4 4.8 %collective-permute-start.28 = (f32[1,2,32,256]{3,2,1,0:T(8,128)S(1)}, f32[1,2,32,256]{3,2,1,0:T(8,128)S(1)}, u32[]{:S(2)}, u32[]{:S(2)}) collective-permute-start(f32[1,2,32,256]{3,2,1,0:T(8,128)S(1)} %get-tuple-element.525), channel_id=1, source_target_pairs={{0,4},{4,8},{8,12},{12,16},{16,20},{20,24},{24,28},{28,0},{1,5},{5... | collective-permute-start | bytes 196616 | tf_op jit(solution)/shard_map/ppermute | solution.py:50
  245.5 4.8 %collective-permute-start.27 = (f32[1,2,32,256]{3,2,1,0:T(8,128)S(1)}, f32[1,2,32,256]{3,2,1,0:T(8,128)S(1)}, u32[]{:S(2)}, u32[]{:S(2)}) collective-permute-start(f32[1,2,32,256]{3,2,1,0:T(8,128)S(1)} %get-tuple-element.526), channel_id=1, source_target_pairs={{0,28},{4,0},{8,4},{12,8},{16,12},{20,16},{24,20},{28,24},{1,29},{... | collective-permute-start | bytes 196616 | tf_op jit(solution)/shard_map/ppermute | solution.py:50
  250.3 4.1 %collective-permute-start.30 = (f32[1,2,8,256]{3,2,1,0:T(8,128)S(1)}, f32[1,2,8,256]{3,2,1,0:T(8,128)S(1)}, u32[]{:S(2)}, u32[]{:S(2)}) collective-permute-start(f32[1,2,8,256]{3,2,1,0:T(8,128)S(1)} %get-tuple-element.541), channel_id=1, source_target_pairs={{0,4},{4,8},{8,12},{12,16},{16,20},{20,24},{24,28},{28,0},{1,5},{5... | collective-permute-start | bytes 49160 | tf_op jit(solution)/shard_map/ppermute | solution.py:39
  250.7 3.7 %collective-permute-start.31 = (f32[1,2,8,256]{3,2,1,0:T(8,128)S(1)}, f32[1,2,8,256]{3,2,1,0:T(8,128)S(1)}, u32[]{:S(2)}, u32[]{:S(2)}) collective-permute-start(f32[1,2,8,256]{3,2,1,0:T(8,128)S(1)} %get-tuple-element.542), channel_id=1, source_target_pairs={{4,0},{8,4},{12,8},{16,12},{20,16},{24,20},{28,24},{0,28},{5,1},{9... | collective-permute-start | bytes 49160 | tf_op jit(solution)/shard_map/ppermute | solution.py:42
  254.5 11.7 %collective-permute-start.32 = (f32[1,2,48,256]{3,2,1,0:T(8,128)S(1)}, f32[1,2,48,256]{3,2,1,0:T(8,128)S(1)}, u32[]{:S(2)}, u32[]{:S(2)}) collective-permute-start(f32[1,2,48,256]{3,2,1,0:T(8,128)S(1)} %pad_maximum_fusion.3), channel_id=1, source_target_pairs={{0,3},{1,0},{2,1},{3,2},{4,7},{5,4},{6,5},{7,6},{8,11},{9,8},{10,9... | collective-permute-start | bytes 294920 | tf_op jit(solution)/shard_map/ppermute | solution.py:27
  258.2 6.4 %collective-permute-start.33 = (f32[1,2,48,256]{3,2,1,0:T(8,128)S(1)}, f32[1,2,48,256]{3,2,1,0:T(8,128)S(1)}, u32[]{:S(2)}, u32[]{:S(2)}) collective-permute-start(f32[1,2,48,256]{3,2,1,0:T(8,128)S(1)} %pad_maximum_fusion.3), channel_id=1, source_target_pairs={{0,1},{1,2},{2,3},{3,0},{4,5},{5,6},{6,7},{7,4},{8,9},{9,10},{10,1... | collective-permute-start | bytes 294920 | tf_op jit(solution)/shard_map/ppermute | solution.py:25
  264.6 6.4 %collective-permute-start.34 = (f32[1,2,48,256]{3,2,1,0:T(8,128)S(1)}, f32[1,2,48,256]{3,2,1,0:T(8,128)S(1)}, u32[]{:S(2)}, u32[]{:S(2)}) collective-permute-start(f32[1,2,48,256]{3,2,1,0:T(8,128)S(1)} %collective-permute-done.33), channel_id=1, source_target_pairs={{0,1},{1,2},{2,3},{3,0},{4,5},{5,6},{6,7},{7,4},{8,9},{9,10},{10,1... | collective-permute-start | bytes 294920 | tf_op jit(solution)/shard_map/ppermute | solution.py:25
